TPU v7x, 512 devices: a whole 4x8x8 slice. The times are simulated.
512 devices in a mesh: ctx: 64 (over z, y_hi, x), head: 8 (over y_lo, core).
Axes of the slice: x: 4, y: 8 (y_hi: 2, y_lo: 4; y = y_hi * 4 + y_lo), z: 8, core: 2. Of those that a mesh axis runs over, the one named last changes fastest.
Arguments:
- hidden: bfloat16 [32768, 4096], P('ctx', 'head'), may hold values from -6 to 6
- w_query: bfloat16 [4096, 2048], P(None, 'head'), may hold values from -0.09375 to 0.09375
- keys: bfloat16 [32768, 2048], P('ctx', 'head'), may hold values from -6 to 6
- values: bfloat16 [32768, 2048], P('ctx', 'head'), may hold values from -6 to 6
- d_out: bfloat16 [32768, 2048], P('ctx', 'head'), may hold values from -6 to 6
- log_decay: float32 [32768, 16], P('ctx', 'head'), may hold values from -1.5 to 0, as said below
Outputs:
- d_hidden: bfloat16 [32768, 4096], P('ctx', 'head')
- d_keys: bfloat16 [32768, 2048], P('ctx', 'head')
- d_values: bfloat16 [32768, 2048], P('ctx', 'head')
Inputs may be any that keep to these rules, and one draw needn't show every extreme that they name: `log_decay`: every entry is negative.
All inputs are finite; a program needn't handle non-finite values.
Results may differ from a plain program's by a relative error of at most 0.013.
Values may be sent and summed in bfloat16 or wider, within the bound.
A program may use at most 64 MiB of HBM per device.

v0:
```python
import jax
import jax.numpy as jnp
from jax import lax
from jax.sharding import PartitionSpec as P

HDIM = 128


highest = lax.Precision.HIGHEST


def carried_in(part, axis, combine, identity, reverse):
    count = lax.axis_size(axis)
    place = lax.axis_index(axis)
    ahead = count - 1 - place if reverse else place
    gathered = jax.tree.map(lambda a: lax.all_gather(a, axis), part)
    state = jax.tree.map(lambda a, e: jnp.zeros_like(a) + jnp.asarray(e, a.dtype), part, identity)

    def one(hop, state):
        source = count - 1 - hop if reverse else hop
        return combine(
            state, jax.tree.map(lambda a: lax.dynamic_index_in_dim(a, source, 0, False), gathered)
        )

    return lax.fori_loop(0, ahead, one, state)


def chain_step(earlier, later):
    return (earlier[0] + later[0], jnp.exp(later[0])[:, None, None] * earlier[1] + later[1])


def summaries(query_heads, scaled_keys, value_heads, grad_heads, cumulative, block_total, scaling):
    keep_share = jnp.exp(block_total[None] - cumulative)[:, :, None]
    decayed_keys = (keep_share * scaled_keys).astype(jnp.bfloat16)
    local_state = jnp.einsum(
        "bhe,bhf->hef", decayed_keys, value_heads, preferred_element_type=jnp.float32
    )
    decayed_queries = (scaling * jnp.exp(cumulative)[:, :, None] * query_heads).astype(jnp.bfloat16)
    local_adjoint = jnp.einsum(
        "bhe,bhf->hef", decayed_queries, grad_heads, preferred_element_type=jnp.float32
    )
    return (local_state, local_adjoint)


def gradients(
    query_heads,
    scaled_keys,
    value_heads,
    grad_heads,
    gate_gain,
    cumulative,
    block_total,
    state_in,
    adjoint_in,
    scaling,
):
    row_count = query_heads.shape[0]
    places = jnp.arange(row_count)
    causal = (places[:, None] >= places[None, :])[None]
    cumul_heads = cumulative.T
    spread = cumul_heads[:, :, None] - cumul_heads[:, None, :]
    decays = jnp.where(causal, jnp.exp(jnp.where(causal, spread, 0.0)), 0.0) * scaling
    weight_dv = (
        decays
        * jnp.einsum("the,she->hts", grad_heads, value_heads, preferred_element_type=jnp.float32)
    ).astype(jnp.bfloat16)
    weight_kq = (
        decays
        * jnp.einsum("the,she->hts", query_heads, scaled_keys, preferred_element_type=jnp.float32)
    ).astype(jnp.bfloat16)
    carry_query = jnp.einsum(
        "thf,hef->the", grad_heads.astype(jnp.float32), state_in, precision=highest
    )
    d_query = (
        jnp.einsum("hts,she->the", weight_dv, scaled_keys, preferred_element_type=jnp.float32)
        + scaling * jnp.exp(cumulative)[:, :, None] * carry_query
    )
    tail_decay = jnp.exp(block_total[None] - cumulative)[:, :, None]
    carry_keys = jnp.einsum(
        "shf,hef->she", value_heads.astype(jnp.float32), adjoint_in, precision=highest
    )
    carry_values = jnp.einsum(
        "she,hef->shf", scaled_keys.astype(jnp.float32), adjoint_in, precision=highest
    )
    d_scaled = (
        jnp.einsum("hts,the->she", weight_dv, query_heads, preferred_element_type=jnp.float32)
        + tail_decay * carry_keys
    )
    d_values = (
        jnp.einsum("hts,the->she", weight_kq, grad_heads, preferred_element_type=jnp.float32)
        + tail_decay * carry_values
    )
    d_keys = gate_gain[:, :, None] * d_scaled
    return (
        d_query.astype(jnp.bfloat16),
        d_keys.astype(jnp.bfloat16),
        d_values.astype(jnp.bfloat16),
    )


def body(hidden, w_query, keys, values, d_out, log_decay):
    row_count = hidden.shape[0]
    head_count = log_decay.shape[1]
    width = w_query.shape[1]
    scaling = HDIM ** (-0.5)
    head_shape = (row_count, head_count, HDIM)
    weight_rows = w_query
    projected = jnp.dot(
        lax.all_gather(hidden, "head", axis=1, tiled=True),
        weight_rows,
        preferred_element_type=jnp.float32,
    )
    query_heads = projected.astype(jnp.bfloat16).reshape(head_shape)
    gate_gain = jnp.sqrt(-jnp.expm1(2.0 * log_decay))
    scaled_keys = (gate_gain[:, :, None] * keys.reshape(head_shape)).astype(jnp.bfloat16)
    value_heads = values.reshape(head_shape)
    grad_heads = d_out.reshape(head_shape)
    cumulative = jnp.cumsum(log_decay, axis=0)
    block_total = cumulative[-1]
    local_state, local_adjoint = summaries(
        query_heads, scaled_keys, value_heads, grad_heads, cumulative, block_total, scaling
    )
    zero_logs = jnp.zeros((head_count,), jnp.float32)
    zero_states = jnp.zeros((head_count, HDIM, HDIM), jnp.float32)
    _, state_in = carried_in(
        (block_total, local_state), "ctx", chain_step, (zero_logs, zero_states), False
    )
    _, adjoint_in = carried_in(
        (block_total, local_adjoint), "ctx", chain_step, (zero_logs, zero_states), True
    )
    d_query, d_keys, d_values = gradients(
        query_heads,
        scaled_keys,
        value_heads,
        grad_heads,
        gate_gain,
        cumulative,
        block_total,
        state_in,
        adjoint_in,
        scaling,
    )
    d_flat = d_query.reshape(row_count, width)
    weight_rows = w_query
    reduced = lax.psum_scatter(
        lax.dot_general(
            weight_rows, d_flat, (((1,), (1,)), ((), ())), preferred_element_type=jnp.float32
        ).astype(jnp.bfloat16),
        "head",
        scatter_dimension=0,
        tiled=True,
    ).astype(jnp.float32)
    d_hidden = reduced.T.astype(jnp.bfloat16)
    return (d_hidden, d_keys.reshape(row_count, width), d_values.reshape(row_count, width))


def solution(mesh):
    return jax.shard_map(
        body,
        mesh=mesh,
        in_specs=(
            P("ctx", "head"),
            P(None, "head"),
            P("ctx", "head"),
            P("ctx", "head"),
            P("ctx", "head"),
            P("ctx", "head"),
        ),
        out_specs=(P("ctx", "head"), P("ctx", "head"), P("ctx", "head")),
        check_vma=False,
    )
```

profile of v0, /device:TPU:1, one launch (start us, length us, event | category | flops | bytes accessed | tf_op | source)
XLA Modules:
  0.0 569.8 jit_solution(13387046657851015726)
XLA Ops:
  9.7 1.1 copy.82
  13.7 57.3 %all-gather.7.cloned.1.call-done = bf16[512,4096]{1,0:T(8,128)(2,1)} async-done(((bf16[512,512]{1,0:T(8,128)(2,1)}), bf16[512,4096]{1,0:T(8,128)(2,1)}) %all-gather.7.cloned.1.call-update) | async-done | bytes 4194320 | tf_op jit(solution)/shard_map/all_gather | solution.py:109
  70.9 3.5 convolution_convert_fusion.1
  76.1 204.5 %all-gather.2 = f32[64,1,2]{2,1,0:T(1,128)S(1)} all-gather(f32[1,1,2]{2,1,0:T(1,128)S(1)} %bitcast.132), channel_id=1, replica_groups=mesh['ctx'=64,'head'=8] {'ctx'}, dimensions={0}, use_global_device_ids=true | all-gather | bytes 520 | tf_op jit(solution)/shard_map/all_gather | solution.py:16
  282.1 1.9 multiply_convert_fusion.1
  284.4 1.4 fusion.10
  285.9 3.3 fusion
  289.2 3.1 fusion.2
  292.2 155.7 %all-gather.11.cloned.1.call-done = f32[128,128,128]{2,1,0:T(8,128)} async-done(((f32[2,128,128]{2,1,0:T(8,128)}), f32[128,128,128]{2,1,0:T(8,128)}) %all-gather.11.cloned.1.call-update) | async-done | bytes 8388624 | tf_op jit(solution)/shard_map/all_gather | solution.py:16
  448.0 107.9 %while.27 = (s32[]{:T(128)}, f32[2,128,128]{2,1,0:T(8,128)S(1)}, s32[]{:T(128)}, f32[64,2]{1,0:T(8,128)}, f32[64,2,128,128]{3,2,1,0:T(8,128)}, /*index=5*/s32[]{:T(128)}, s32[]{:T(128)}, s32[]{:T(128)}, s32[]{:T(128)}) while((s32[]{:T(128)}, f32[2,128,128]{2,1,0:T(8,128)S(1)}, s32[]{:T(128)}, f32[64,2]{1,0:T(8,128)}, ...), condition=%wide.region_6.7_spmd, body=%wide.region_5.6_spmd.sunk | while | flops 65542 | bytes 393387 | solution.py:25
  448.7 1.0 bitcast_add_fusion.5
  450.4 1.0 bitcast_add_fusion.5
  452.1 1.0 bitcast_add_fusion.5
  453.8 1.0 bitcast_add_fusion.5
  455.5 1.0 bitcast_add_fusion.5
  457.2 1.0 bitcast_add_fusion.5
  458.9 1.0 bitcast_add_fusion.5
  460.6 1.0 bitcast_add_fusion.5
  462.4 1.0 bitcast_add_fusion.5
  464.1 1.0 bitcast_add_fusion.5
  465.8 1.0 bitcast_add_fusion.5
  467.5 1.0 bitcast_add_fusion.5
  469.2 1.0 bitcast_add_fusion.5
  470.9 1.0 bitcast_add_fusion.5
  472.6 1.0 bitcast_add_fusion.5
  474.4 1.0 bitcast_add_fusion.5
  476.1 1.0 bitcast_add_fusion.5
  477.8 1.0 bitcast_add_fusion.5
  479.5 1.0 bitcast_add_fusion.5
  481.2 1.0 bitcast_add_fusion.5
  482.9 1.0 bitcast_add_fusion.5
  484.6 1.0 bitcast_add_fusion.5
  486.3 1.0 bitcast_add_fusion.5
  488.0 1.0 bitcast_add_fusion.5
  489.7 1.0 bitcast_add_fusion.5
  491.5 1.0 bitcast_add_fusion.5
  493.2 1.0 bitcast_add_fusion.5
  494.9 1.0 bitcast_add_fusion.5
  496.6 1.0 bitcast_add_fusion.5
  498.4 1.0 bitcast_add_fusion.5
  500.1 1.0 bitcast_add_fusion.5
  501.8 1.0 bitcast_add_fusion.5
  503.5 1.0 bitcast_add_fusion.5
  505.2 1.0 bitcast_add_fusion.5
  507.0 1.0 bitcast_add_fusion.5
  508.7 1.0 bitcast_add_fusion.5
  510.4 1.0 bitcast_add_fusion.5
  512.1 1.0 bitcast_add_fusion.5
  513.8 1.0 bitcast_add_fusion.5
  515.5 1.0 bitcast_add_fusion.5
  517.3 1.0 bitcast_add_fusion.5
  519.0 1.0 bitcast_add_fusion.5
  520.7 1.0 bitcast_add_fusion.5
  522.4 1.0 bitcast_add_fusion.5
  524.1 1.0 bitcast_add_fusion.5
  525.8 1.0 bitcast_add_fusion.5
  527.5 1.0 bitcast_add_fusion.5
  530.9 1.0 bitcast_add_fusion.5
  534.3 1.0 bitcast_add_fusion.5
  549.8 1.0 bitcast_add_fusion.5
  555.9 2.2 fusion.11
  558.1 1.8 copy.98
  559.9 1.3 fusion.7
  561.2 1.3 fusion.12
  (121 shorter events, 66.1 us)
Async XLA Ops:
  7.2 63.8 %copy-start = (bf16[4096,256]{1,0:T(8,128)(2,1)S(1)}, bf16[4096,256]{1,0:T(8,128)(2,1)}, u32[]{:S(2)}) copy-start(bf16[4096,256]{1,0:T(8,128)(2,1)} %param.11) | copy-start | bytes 6291460
  7.2 5.4 copy-start.4
  7.2 6.3 %copy-start.5 = (bf16[512,256]{1,0:T(8,128)(2,1)S(1)}, bf16[512,256]{1,0:T(8,128)(2,1)}, u32[]{:S(2)}) copy-start(bf16[512,256]{1,0:T(8,128)(2,1)} %param.14) | copy-start | bytes 786436
  7.2 63.7 %all-gather.7.cloned.1.call-start = ((), (), s32[]{:S(2)}) async-start(), calls=%async_computation.2 | async-start | bytes 4718592 | tf_op jit(solution)/shard_map/all_gather | solution.py:109
  7.9 276.1 %all-gather.9.cloned.1.call-start = ((), (), s32[]{:S(2)}) async-start(), calls=%async_computation.3 | async-start | bytes 8519680 | tf_op jit(solution)/shard_map/all_gather | solution.py:16
  11.8 0.7 copy-start.1
  13.5 434.5 %all-gather.11.cloned.1.call-start = ((), (), s32[]{:S(2)}) async-start(), calls=%async_computation.4 | async-start | bytes 8519680 | tf_op jit(solution)/shard_map/all_gather | solution.py:16
  74.4 0.7 copy-start.3
  76.0 487.3 %reduce-scatter.2.cloned.1.call-start = ((), (), s32[]{:S(2)}) async-start(), calls=%async_computation.1 | async-start | bytes 4718592 | tf_op jit(solution)/shard_map/reduce_scatter | solution.py:145
  281.4 0.7 copy-start.6
  292.2 263.7 %copy-start.2 = (bf16[512,2,128]{0,2,1:T(8,128)(2,1)S(1)}, bf16[512,2,128]{0,2,1:T(8,128)(2,1)}, u32[]{:S(2)}) copy-start(bf16[512,2,128]{0,2,1:T(8,128)(2,1)} %copy-done.1) | copy-start | bytes 786436
Sparse Core Ops, SparseCore 0:
  10.1 60.7 all-gather.6
  76.0 177.9 all-gather.8
  258.4 189.4 all-gather.10
  451.2 55.9 reduce-scatter.1
where the time goes:
time: 578 us; the launch traced here: 570 us
  waiting for transfers between devices  214 us (37%)
  blocking collectives  204 us (35%)
  other arithmetic  64.4 us (11%)
  local copies, waits for them, and re-layouts  51.3 us (9%)
  matrix products  20 us (3%)
  between operations  13.9 us (2%)
    all_gather x1, blocking collectives, carried_in(): gathered = jax.tree.map(lambda a: lax.all_gather(a, axis), part)  204 us
    all_gather x2, waiting for transfers between devices, carried_in(): gathered = jax.tree.map(lambda a: lax.all_gather(a, axis), part)  156 us
    add x63, other arithmetic, chain_step(): jnp.exp(later[0])[:, None, None] * earlier[1] + later[1]  62.7 us
    all_gather x1, waiting for transfers between devices, body(): lax.all_gather(hidden, 'head', axis=1, tiled=True)  57.3 us
    exp x63, local copies, waits for them, and re-layouts, chain_step(): jnp.exp(later[0])[:, None, None] * earlier[1] + later[1]  43.4 us
  transfers between devices with their start and end apart: 4, of which 2 were waited for; matrix products, arithmetic and copies ran while one was open for 23% of the time, Pallas kernels for 0%

commit v1 on v0

v1 whole, which is shorter than its diff:
```python
import functools

import jax
import jax.numpy as jnp
from jax import lax
from jax.experimental import pallas as pl
from jax.experimental.pallas import tpu as pltpu
from jax.sharding import PartitionSpec as P

MESH = pl.DeviceIdType.MESH
F32 = jnp.float32
BF16 = jnp.bfloat16
HDIM = 128
NX, NY, NZ = 4, 2, 8
NP = 4
QUARTER = HDIM // NX
OFFSETS = (2, -2, 1, -1)
AHEAD = 3


def mm(a, b):
    return lax.dot_general(a, b, (((1,), (0,)), ((), ())), preferred_element_type=F32)


def mm_nt(a, b):
    return lax.dot_general(a, b, (((1,), (1,)), ((), ())), preferred_element_type=F32)


def mm_tn(a, b):
    return lax.dot_general(a, b, (((0,), (0,)), ((), ())), preferred_element_type=F32)


def one_less_exp(x):
    series = jnp.full_like(x, 1.0)
    for n in range(9, 1, -1):
        series = 1.0 + x * (1.0 / n) * series
    return jnp.where(x > -0.5, -x * series, 1.0 - jnp.exp(x))


def kernel(
    hidden, w_hbm, keys, values, d_out, logs,
    dh_ref, dk_ref, dv_ref,
    hid, w, wr, dqf, query, sk, lg, rows, dec, wdv,
    loc, p1, p2, p3, p4s, p4, tx, by, bz, sums,
    in_sem,
    h_send, h_sib, h_fwd, h_rel, h_recv,
    q_send, q_sib, q_fwd, q_rel, q_recv,
    wy_send, wy_recv, wz_send, wz_recv, wx_send, wx_recv, wf_send, wf_recv,
    s1_send, s1_recv, s2_send, s2_recv, s3_send, s3_recv, s4_send, s4_recv,
    t1_send, t1_recv, t2_send, t2_recv, t3_send, t3_recv,
):
    scale = HDIM ** (-0.5)
    tokens = hidden.shape[0]
    feats = hidden.shape[1]
    width = w_hbm.shape[1]
    nhead = width // HDIM
    ctx, head = lax.axis_index("ctx"), lax.axis_index("head")
    x = lax.rem(ctx, NX)
    y = lax.rem(lax.div(ctx, NX), NY)
    z = lax.div(ctx, NX * NY)
    chip, core = lax.div(head, 2), lax.rem(head, 2)
    sib = 2 * chip + 1 - core

    def ctx_at(zz, yy, xx):
        return (zz * NY + yy) * NX + xx

    def to_head(other):
        return {"head": other}

    def to_ctx(other):
        return {"ctx": other}

    def remote(src, dst, send, recv, device):
        return pltpu.make_async_remote_copy(
            src_ref=src, dst_ref=dst, send_sem=send, recv_sem=recv,
            device_id=device, device_id_type=MESH,
        )

    def arrived(dst, sem):
        remote(dst, dst, sem, sem, to_head(sib)).wait_recv()

    pending = []

    def send(copy):
        copy.start()
        pending.append((None, copy))

    def send_if(cond, make):
        @pl.when(cond)
        def _():
            make().start()

        pending.append((cond, make))

    local = [
        pltpu.make_async_copy(hidden, hid.at[head], in_sem.at[0]),
        pltpu.make_async_copy(w_hbm, w, in_sem.at[1]),
    ]
    for copy in local:
        copy.start()

    barrier = pltpu.get_barrier_semaphore()
    partners = [to_head(lax.rem(head + d, 2 * NP)) for d in range(1, 2 * NP)]
    partners += [to_ctx(ctx_at(z, y, lax.rem(x + d, NX))) for d in range(1, NX)]
    partners += [to_ctx(ctx_at(z, 1 - y, x))]
    partners += [to_ctx(ctx_at(lax.rem(z + d, NZ), y, x)) for d in range(1, NZ)]
    for partner in partners:
        pl.semaphore_signal(barrier, inc=1, device_id=partner, device_id_type=MESH)
    pl.semaphore_wait(barrier, len(partners))

    part = feats // (NX * NZ)
    slot = pl.multiple_of((x * NZ + z) * part, part)

    def weights_y():
        local[1].wait()
        mine = w.at[pl.ds(pl.multiple_of(head * feats + slot, part), part), :]
        for d in range(1, 2 * NP):
            other = lax.rem(head + d, 2 * NP)
            send(remote(
                w.at[pl.ds(pl.multiple_of(other * feats + slot, part), part), :],
                wr.at[head, pl.ds(slot, part), :],
                wy_send.at[d - 1], wy_recv.at[head], to_head(other),
            ))
        wr[head, pl.ds(slot, part), :] = mine[...]

    def weights_z():
        for d in range(1, 2 * NP):
            other = lax.rem(head + d, 2 * NP)
            arrived(wr.at[other, pl.ds(slot, part), :], wy_recv.at[other])
        mine = wr.at[:, pl.ds(slot, part), :]
        for d in (4, 3, 5, 2, 6, 1, 7):
            send(remote(mine, mine, wz_send.at[d - 1], wz_recv.at[z],
                        to_ctx(ctx_at(lax.rem(z + d, NZ), y, x))))

    line = part * NZ
    right, left = lax.rem(x + 1, NX), lax.rem(x + NX - 1, NX)
    across = lax.rem(x + 2, NX)

    def line_of(xx):
        return pl.ds(pl.multiple_of(xx * line, line), line)

    def weights_x():
        for d in range(1, NZ):
            zz = lax.rem(z + d, NZ)
            arrived(wr.at[:, pl.ds(pl.multiple_of((x * NZ + zz) * part, part), part), :],
                    wz_recv.at[zz])
        mine = wr.at[:, line_of(x), :]
        send(remote(mine, mine, wx_send.at[0], wx_recv.at[0], to_ctx(ctx_at(z, y, right))))
        send(remote(mine, mine, wx_send.at[1], wx_recv.at[1], to_ctx(ctx_at(z, y, left))))

    def weights_forward():
        from_left = wr.at[:, line_of(left), :]
        arrived(from_left, wx_recv.at[0])
        half = wr.at[pl.ds(0, NP), line_of(left), :]
        send(remote(half, half, wf_send.at[0], wf_recv.at[0], to_ctx(ctx_at(z, y, right))))
        from_right = wr.at[:, line_of(right), :]
        arrived(from_right, wx_recv.at[1])
        half = wr.at[pl.ds(NP, NP), line_of(right), :]
        send(remote(half, half, wf_send.at[1], wf_recv.at[1], to_ctx(ctx_at(z, y, left))))

    def weights_end():
        arrived(wr.at[pl.ds(0, NP), line_of(across), :], wf_recv.at[0])
        arrived(wr.at[pl.ds(NP, NP), line_of(across), :], wf_recv.at[1])

    def gather(buf, step, s_send, s_sib, s_fwd, s_rel, s_recv):
        def piece(block, k):
            return buf.at[block, pl.ds(k * step, step), :]

        def issue(k):
            mine = piece(head, k)
            recv = s_recv.at[head, k]
            for i, d in enumerate(OFFSETS):
                other = chip + d
                ok = jnp.logical_and(other >= 0, other < NP)
                send_if(ok, functools.partial(
                    remote, mine, mine, s_send.at[i, k], recv, to_head(2 * other + core)))
            send(remote(mine, mine, s_sib.at[k], recv, to_head(sib)))

        def forward(k):
            for i, d in enumerate((2, 1, 3)):
                block = 2 * lax.rem(chip + d, NP) + core
                got = piece(block, k)
                recv = s_recv.at[block, k]
                arrived(got, recv)
                if d == 2:
                    ok = jnp.logical_and(chip >= 1, chip <= 2)
                    end = jnp.where(chip == 2, 3, 0)
                    send_if(ok, functools.partial(
                        remote, got, got, s_rel.at[k], recv, to_head(2 * end + core)))
                send(remote(got, got, s_fwd.at[i, k], recv, to_head(sib)))

        def finish(k):
            for d in range(NP):
                block = 2 * lax.rem(chip + d, NP) + 1 - core
                arrived(piece(block, k), s_recv.at[block, k])

        return issue, forward, finish

    h_step = tokens // h_sib.shape[0]
    q_step = tokens // q_sib.shape[0]
    h_issue, h_forward, h_finish = gather(hid, h_step, h_send, h_sib, h_fwd, h_rel, h_recv)
    q_issue, q_forward, q_finish = gather(dqf, q_step, q_send, q_sib, q_fwd, q_rel, q_recv)

    def line_fold(parts, gains, reverse, start):
        outs = [None] * len(parts)
        acc = start
        order = range(len(parts))
        for i in reversed(order) if reverse else order:
            outs[i] = acc
            acc = [gains[i][h] * acc[h] + parts[i][h] for h in range(nhead)]
        return outs, acc

    def zeros():
        return [jnp.zeros((QUARTER, HDIM), F32) for _ in range(nhead)]

    def gains_of(ref, count):
        return [[jnp.exp(ref[i][h : h + 1, :]) for h in range(nhead)] for i in range(count)]

    def parts_of(ref, n, count):
        return [[ref[n, i, h].astype(F32) for h in range(nhead)] for i in range(count)]

    def scan_x(n, states):
        for q in range(NX):
            for h in range(nhead):
                loc[n, q, h] = states[h][q * QUARTER : (q + 1) * QUARTER].astype(BF16)
        for d in (2, 1, 3):
            xx = lax.rem(x + d, NX)
            device = to_ctx(ctx_at(z, y, xx))
            send(remote(loc.at[n, xx], p1.at[n, x], s1_send.at[n, d - 1], s1_recv.at[n, x], device))
            if n == 0:
                send(remote(tx.at[x], tx.at[x], t1_send.at[d - 1], t1_recv.at[x], device))
        p1[n, x] = loc[n, x]

    def scan_y(n):
        for d in (1, 3, 2):
            xx = lax.rem(x + d, NX)
            arrived(p1.at[n, xx], s1_recv.at[n, xx])
            if n == 0:
                arrived(tx.at[xx], t1_recv.at[xx])
        if n == 0:
            by[y] = tx[0] + tx[1] + tx[2] + tx[3]
        _, total = line_fold(parts_of(p1, n, NX), gains_of(tx, NX), n == 1, zeros())
        for h in range(nhead):
            p2[n, y, h] = total[h].astype(BF16)
        device = to_ctx(ctx_at(z, 1 - y, x))
        send(remote(p2.at[n, y], p2.at[n, y], s2_send.at[n], s2_recv.at[n, y], device))
        if n == 0:
            send(remote(by.at[y], by.at[y], t2_send.at[0], t2_recv.at[y], device))

    def scan_z(n):
        arrived(p2.at[n, 1 - y], s2_recv.at[n, 1 - y])
        if n == 0:
            arrived(by.at[1 - y], t2_recv.at[1 - y])
            bz[z] = by[0] + by[1]
        _, total = line_fold(parts_of(p2, n, NY), gains_of(by, NY), n == 1, zeros())
        for h in range(nhead):
            p3[n, z, h] = total[h].astype(BF16)
        for d in (4, 3, 5, 2, 6, 1, 7):
            device = to_ctx(ctx_at(lax.rem(z + d, NZ), y, x))
            send(remote(p3.at[n, z], p3.at[n, z], s3_send.at[n, d - 1], s3_recv.at[n, z], device))
            if n == 0:
                send(remote(bz.at[z], bz.at[z], t3_send.at[d - 1], t3_recv.at[z], device))

    def scan_back(n):
        for d in (1, 7, 2, 6, 3, 5, 4):
            zz = lax.rem(z + d, NZ)
            arrived(p3.at[n, zz], s3_recv.at[n, zz])
            if n == 0:
                arrived(bz.at[zz], t3_recv.at[zz])
        reverse = n == 1
        gains = gains_of(bz, NZ)
        parts = parts_of(p3, n, NZ)
        acc = zeros()
        for i in reversed(range(NZ)) if reverse else range(NZ):
            use = z < i if reverse else z > i
            keep = jnp.where(use, 1.0, 0.0)
            acc = [
                acc[h] * (1.0 - keep + keep * gains[i][h]) + keep * parts[i][h]
                for h in range(nhead)
            ]
        outs, _ = line_fold(parts_of(p2, n, NY), gains_of(by, NY), reverse, acc)
        first = jnp.where(y == 0, 1.0, 0.0)
        acc = [first * outs[0][h] + (1.0 - first) * outs[1][h] for h in range(nhead)]
        outs, _ = line_fold(parts_of(p1, n, NX), gains_of(tx, NX), reverse, acc)
        for i in range(NX):
            for h in range(nhead):
                p4s[n, i, h] = outs[i][h].astype(BF16)
        for d in (2, 1, 3):
            xx = lax.rem(x + d, NX)
            send(remote(p4s.at[n, xx], p4.at[n, x], s4_send.at[n, d - 1], s4_recv.at[n, x],
                        to_ctx(ctx_at(z, y, xx))))
        p4[n, x] = p4s[n, x]

    def scan_end(n):
        for d in (1, 3, 2):
            xx = lax.rem(x + d, NX)
            arrived(p4.at[n, xx], s4_recv.at[n, xx])
        return [
            jnp.concatenate([p4[n, q, h] for q in range(NX)], axis=0) for h in range(nhead)
        ]

    def cols(h):
        return slice(h * HDIM, (h + 1) * HDIM)

    weights_y()
    local[0].wait()
    for k in range(AHEAD):
        h_issue(k)

    lg[...] = jnp.zeros_like(lg)
    lg[0:nhead, :] = logs[...]
    log_rows = lg[...]
    gate = jnp.sqrt(one_less_exp(2.0 * log_rows))
    lane = lax.broadcasted_iota(jnp.int32, log_rows.shape, 1)
    cumul = log_rows
    shift = 1
    while shift < tokens:
        cumul = cumul + jnp.where(lane >= shift, pltpu.roll(cumul, shift, 1), 0.0)
        shift *= 2
    total = cumul[:, tokens - 1 : tokens]
    tx[x] = jnp.broadcast_to(total, (8, HDIM))
    rows[0:8, :] = gate
    rows[8:16, :] = scale * jnp.exp(cumul)
    rows[16:24, :] = jnp.exp(total - cumul)
    rows[24:32, :] = cumul
    columns = jnp.transpose(rows[...])
    gate_c = [columns[:, h : h + 1] for h in range(nhead)]
    head_c = [columns[:, 8 + h : 9 + h] for h in range(nhead)]
    tail_c = [columns[:, 16 + h : 17 + h] for h in range(nhead)]
    cumul_c = [columns[:, 24 + h : 25 + h] for h in range(nhead)]

    states = []
    for h in range(nhead):
        scaled = (gate_c[h] * keys[:, cols(h)].astype(F32)).astype(BF16)
        sk[:, cols(h)] = scaled
        decayed = (tail_c[h] * scaled.astype(F32)).astype(BF16)
        states.append(mm_tn(decayed, values[:, cols(h)]))
    scan_x(0, states)
    weights_z()

    block = 128
    tri = lax.broadcasted_iota(jnp.int32, (block, block), 0) >= lax.broadcasted_iota(
        jnp.int32, (block, block), 1
    )
    for h in range(nhead):
        cumul_r = rows[24 + h : 25 + h, :]
        for t0 in range(0, tokens, block):
            t = slice(t0, t0 + block)
            for s0 in range(0, t0 + block, block):
                s = slice(s0, s0 + block)
                spread = cumul_c[h][t] - cumul_r[:, s]
                if s0 == t0:
                    decays = jnp.where(tri, jnp.exp(jnp.where(tri, spread, 0.0)) * scale, 0.0)
                else:
                    decays = jnp.exp(spread) * scale
                dots = mm_nt(d_out[t, cols(h)], values[s, cols(h)])
                dec[h, t, s] = decays
                wdv[h, t, s] = (decays * dots).astype(BF16)

    def intra_query(h, t0):
        t = slice(t0, t0 + block)
        return mm(wdv[h, t, 0 : t0 + block], sk[0 : t0 + block, cols(h)])

    scan_y(0)

    def h_product(k0, k1):
        for k in range(k0, k1):
            h_finish(k)
        t = slice(k0 * h_step, k1 * h_step)
        acc = jnp.zeros((t.stop - t.start, width), F32)
        for b in range(2 * NP):
            acc = acc + mm(hid[b, t, :], w[b * feats : (b + 1) * feats, :])
        query[t, :] = acc.astype(BF16)

    chunks = h_sib.shape[0]

    def h_chunk(k):
        h_forward(k)
        if k + AHEAD < chunks:
            h_issue(k + AHEAD)

    h_chunk(0)
    h_chunk(1)
    scan_z(0)
    h_product(0, 2)
    h_chunk(2)
    weights_x()
    h_chunk(3)
    h_product(2, 4)
    h_chunk(4)
    scan_back(0)
    h_chunk(5)
    h_product(4, 6)
    h_chunk(6)
    weights_forward()
    h_chunk(7)
    state_in = scan_end(0)
    h_product(6, 8)

    adjoints = []
    for h in range(nhead):
        decayed = (head_c[h] * query[:, cols(h)].astype(F32)).astype(BF16)
        adjoints.append(mm_tn(decayed, d_out[:, cols(h)]))
    scan_x(1, adjoints)

    for h in range(nhead):
        for t0 in range(0, tokens, block):
            t = slice(t0, t0 + block)
            carry = mm_nt(d_out[t, cols(h)], state_in[h])
            out = intra_query(h, t0) + head_c[h][t] * carry
            dqf[head, t, cols(h)] = out.astype(BF16)

    scan_y(1)
    q_chunks = q_sib.shape[0]
    for k in range(q_chunks):
        q_issue(k)

    for h in range(nhead):
        for s0 in range(0, tokens, block):
            s = slice(s0, s0 + block)
            later = slice(s0, tokens)
            scores = mm_nt(query[later, cols(h)], sk[s, cols(h)])
            weight = (dec[h, later, s] * scores).astype(BF16)
            sums[0, s, cols(h)] = mm_tn(wdv[h, later, s], query[later, cols(h)])
            sums[1, s, cols(h)] = mm_tn(weight, d_out[later, cols(h)])

    scan_z(1)
    q_forward(0)
    weights_end()
    q_forward(1)
    scan_back(1)
    q_forward(2)
    q_forward(3)
    adjoint_in = scan_end(1)
    for h in range(nhead):
        carry_keys = mm_nt(values[:, cols(h)], adjoint_in[h])
        carry_values = mm(sk[:, cols(h)], adjoint_in[h])
        d_scaled = sums[0, :, cols(h)] + tail_c[h] * carry_keys
        dk_ref[:, cols(h)] = (gate_c[h] * d_scaled).astype(BF16)
        dv_ref[:, cols(h)] = (sums[1, :, cols(h)] + tail_c[h] * carry_values).astype(BF16)
    for k in range(q_chunks):
        q_finish(k)
        t = slice(k * q_step, (k + 1) * q_step)
        acc = jnp.zeros((q_step, feats), F32)
        for b in range(2 * NP):
            acc = acc + mm_nt(dqf[b, t, :], wr[b])
        dh_ref[t, :] = acc.astype(BF16)

    for cond, copy in pending:
        if cond is None:
            copy.wait_send()
        else:
            @pl.when(cond)
            def _(copy=copy):
                copy().wait_send()


def body(hidden, w_query, keys, values, d_out, log_decay):
    tokens, feats = hidden.shape
    width = w_query.shape[1]
    nhead = width // HDIM
    groups = 2 * NP
    h_chunks, q_chunks = 8, 4
    dma = pltpu.SemaphoreType.DMA
    vmem = pltpu.VMEM
    scratch = [
        vmem((groups, tokens, feats), BF16),
        vmem(w_query.shape, BF16),
        vmem((groups, feats, width), BF16),
        vmem((groups, tokens, width), BF16),
        vmem((tokens, width), BF16),
        vmem((tokens, width), BF16),
        vmem((8, tokens), F32),
        vmem((128, tokens), F32),
        vmem((nhead, tokens, tokens), F32),
        vmem((nhead, tokens, tokens), BF16),
        vmem((2, NX, nhead, QUARTER, HDIM), BF16),
        vmem((2, NX, nhead, QUARTER, HDIM), BF16),
        vmem((2, NY, nhead, QUARTER, HDIM), BF16),
        vmem((2, NZ, nhead, QUARTER, HDIM), BF16),
        vmem((2, NX, nhead, QUARTER, HDIM), BF16),
        vmem((2, NX, nhead, QUARTER, HDIM), BF16),
        vmem((NX, 8, HDIM), F32),
        vmem((NY, 8, HDIM), F32),
        vmem((NZ, 8, HDIM), F32),
        vmem((2, tokens, width), F32),
        dma((2,)),
    ]
    for chunks in (h_chunks, q_chunks):
        scratch += [dma((4, chunks)), dma((chunks,)), dma((3, chunks)), dma((chunks,)),
                    dma((groups, chunks))]
    scratch += [dma((groups - 1,)), dma((groups,)), dma((NZ - 1,)), dma((NZ,)),
                dma((2,)), dma((2,)), dma((2,)), dma((2,))]
    scratch += [dma((2, NX - 1)), dma((2, NX)), dma((2,)), dma((2, NY)),
                dma((2, NZ - 1)), dma((2, NZ)), dma((2, NX - 1)), dma((2, NX))]
    scratch += [dma((NX - 1,)), dma((NX,)), dma((1,)), dma((NY,)), dma((NZ - 1,)), dma((NZ,))]
    in_vmem = pl.BlockSpec(memory_space=pltpu.VMEM)
    anywhere = pl.BlockSpec(memory_space=pl.ANY)
    return pl.pallas_call(
        kernel,
        out_shape=(
            jax.ShapeDtypeStruct((tokens, feats), BF16),
            jax.ShapeDtypeStruct((tokens, width), BF16),
            jax.ShapeDtypeStruct((tokens, width), BF16),
        ),
        in_specs=[anywhere, anywhere, in_vmem, in_vmem, in_vmem, in_vmem],
        out_specs=(in_vmem, in_vmem, in_vmem),
        scratch_shapes=scratch,
        compiler_params=pltpu.CompilerParams(
            collective_id=0, has_side_effects=True, vmem_limit_bytes=56 * 1024 * 1024
        ),
    )(hidden, w_query, keys, values, d_out, log_decay.T)


def solution(mesh):
    return jax.shard_map(
        body,
        mesh=mesh,
        in_specs=(
            P("ctx", "head"),
            P(None, "head"),
            P("ctx", "head"),
            P("ctx", "head"),
            P("ctx", "head"),
            P("ctx", "head"),
        ),
        out_specs=(P("ctx", "head"), P("ctx", "head"), P("ctx", "head")),
        check_vma=False,
    )
```

time: 578 us -> 89.4 us (0.15); the launches traced: 570 us -> 89.1 us
  waiting for transfers between devices: 214 us -> 0 us
  blocking collectives: 204 us -> 0 us
  Pallas kernels: 0 us -> 83.3 us
  other arithmetic: 64.4 us -> 0 us
  local copies, waits for them, and re-layouts: 51.3 us -> 5.21 us
  matrix products: 20 us -> 0 us
  between operations: 13.9 us -> 0.64 us
    all_gather x3 -> x0, waiting for transfers between devices: 213 us -> none  [the longest x2 156 us: carried_in(): gathered = jax.tree.map(lambda a: lax.all_gather(a, axis), part)]
    all_gather x1 -> x0, blocking collectives: 204 us -> none  [carried_in(): gathered = jax.tree.map(lambda a: lax.all_gather(a, axis), part)]
    pallas_call x0 -> x1, Pallas kernels: none -> 83.3 us  [body(): pl.pallas_call(kernel, out_shape=(jax.ShapeDtypeStruct((tokens, feats), B...]
    add x63 -> x0, other arithmetic: 62.7 us -> none  [chain_step(): jnp.exp(later[0])[:, None, None] * earlier[1] + later[1]]
    exp x63 -> x0, local copies, waits for them, and re-layouts: 43.4 us -> none  [chain_step(): jnp.exp(later[0])[:, None, None] * earlier[1] + later[1]]
    dot_general x11 -> x0, matrix products: 20 us -> none  [the longest x1 3.48 us: body(): jnp.dot(lax.all_gather(hidden, 'head', axis=1, tiled=True), weight_rows,...]
  transfers between devices with their start and end apart: 4 -> 0, of which waited for: 2 -> 0; matrix products, arithmetic and copies ran while one was open for 23% -> 0% of each run, Pallas kernels for 0% -> 0%
where the time goes in v1:
time: 89.4 us; the launch traced here: 89.1 us
  Pallas kernels  83.3 us (93%)
  local copies, waits for them, and re-layouts  5.21 us (6%)
    pallas_call x1, Pallas kernels, body(): pl.pallas_call(kernel, out_shape=(jax.ShapeDtypeStruct((tokens, feats), B...  83.3 us
    unnamed x3, local copies, waits for them, and re-layouts  5.21 us

profile of v1, /device:TPU:1, one launch (start us, length us, event | category | flops | bytes accessed | tf_op | source)
XLA Modules:
  0.0 89.1 jit_solution(12819038694156347715)
XLA Ops:
  0.6 83.3 %shard_map.85 = (bf16[512,512]{1,0:T(8,128)(2,1)}, bf16[512,256]{1,0:T(8,128)(2,1)}, bf16[512,256]{1,0:T(8,128)(2,1)}) custom-call(bf16[512,512]{1,0:T(8,128)(2,1)} %hidden.1, bf16[4096,256]{1,0:T(8,128)(2,1)} %w_hbm.1, bf16[512,256]{1,0:T(8,128)(2,1)} %keys.1, bf16[512,256]{1,0:T(8,128)(2,1)} %values.1, bf16[512,256]{1,0:T(8,128)(2,1)} %d_out.1, ...), custom_call_target="tpu_custom_call" | custom-call | tf_op jit(solution)/shard_map/pallas_call | solution.py:499
  83.9 1.9 %copy.12 = bf16[512,512]{1,0:T(8,128)(2,1)} copy(bf16[512,512]{1,0:T(8,128)(2,1)} %get-tuple-element.6) | data formatting | bytes 1048576
  85.8 1.7 %copy.13 = bf16[512,256]{1,0:T(8,128)(2,1)} copy(bf16[512,256]{1,0:T(8,128)(2,1)} %get-tuple-element.7) | data formatting | bytes 524288
  87.4 1.7 %copy.14 = bf16[512,256]{1,0:T(8,128)(2,1)} copy(bf16[512,256]{1,0:T(8,128)(2,1)} %get-tuple-element.8) | data formatting | bytes 524288

commit v2 on v1

v2 whole, which is shorter than its diff:
```python
import functools

import jax
import jax.numpy as jnp
from jax import lax
from jax.experimental import pallas as pl
from jax.experimental.pallas import tpu as pltpu
from jax.sharding import PartitionSpec as P

MESH = pl.DeviceIdType.MESH
F32 = jnp.float32
BF16 = jnp.bfloat16
HDIM = 128
NX, NY, NZ = 4, 2, 8
NP = 4
QUARTER = HDIM // NX
OFFSETS = (2, -2, 1, -1)
AHEAD = 3


def mm(a, b):
    return lax.dot_general(a, b, (((1,), (0,)), ((), ())), preferred_element_type=F32)


def mm_nt(a, b):
    return lax.dot_general(a, b, (((1,), (1,)), ((), ())), preferred_element_type=F32)


def mm_tn(a, b):
    return lax.dot_general(a, b, (((0,), (0,)), ((), ())), preferred_element_type=F32)


def one_less_exp(x):
    series = jnp.full_like(x, 1.0)
    for n in range(9, 1, -1):
        series = 1.0 + x * (1.0 / n) * series
    return jnp.where(x > -0.5, -x * series, 1.0 - jnp.exp(x))


def kernel(
    hidden, w_hbm, keys_hbm, values_hbm, d_out_hbm, logs_hbm,
    dh_hbm, dk_hbm, dv_hbm,
    logs, keys, values, d_out, dh_ref, dk_ref, dv_ref,
    hid, w, wr, dqf, query, sk, lg, rows, dec, wdv,
    loc, p1, p2, p3, p4s, p4, tx, by, bz, sums,
    in_sem, out_sem,
    h_send, h_recv, h_near,
    q_send, q_recv, q_near,
    wy_send, wy_recv, wz_send, wz_recv, wx_send, wx_recv, wf_send, wf_recv,
    s_send, s_recv, t_send, t_recv,
):
    scale = HDIM ** (-0.5)
    tokens = hidden.shape[0]
    feats = hidden.shape[1]
    width = w_hbm.shape[1]
    nhead = width // HDIM
    ctx, head = lax.axis_index("ctx"), lax.axis_index("head")
    x = lax.rem(ctx, NX)
    y = lax.rem(lax.div(ctx, NX), NY)
    z = lax.div(ctx, NX * NY)
    chip, core = lax.div(head, 2), lax.rem(head, 2)
    sib = 2 * chip + 1 - core

    def ctx_at(zz, yy, xx):
        return (zz * NY + yy) * NX + xx

    def to_head(other):
        return {"head": other}

    def to_ctx(other):
        return {"ctx": other}

    def remote(src, dst, send, recv, device):
        return pltpu.make_async_remote_copy(
            src_ref=src, dst_ref=dst, send_sem=send, recv_sem=recv,
            device_id=device, device_id_type=MESH,
        )

    def arrived(dst, sem):
        remote(dst, dst, sem, sem, to_head(sib)).wait_recv()

    pending = []

    def sent(src, sem, cond=None):
        pending.append((cond, src, sem))

    barrier = pltpu.get_barrier_semaphore()
    partners = [to_head(lax.rem(head + d, 2 * NP)) for d in range(1, 2 * NP)]
    partners += [to_ctx(ctx_at(z, y, lax.rem(x + d, NX))) for d in range(1, NX)]
    partners += [to_ctx(ctx_at(z, 1 - y, x))]
    partners += [to_ctx(ctx_at(lax.rem(z + d, NZ), y, x)) for d in range(1, NZ)]
    for partner in partners:
        pl.semaphore_signal(barrier, inc=1, device_id=partner, device_id_type=MESH)

    local = [
        pltpu.make_async_copy(src, dst, in_sem.at[i])
        for i, (src, dst) in enumerate((
            (hidden, hid.at[head]), (w_hbm, w), (keys_hbm, keys),
            (values_hbm, values), (d_out_hbm, d_out), (logs_hbm, logs),
        ))
    ]
    lg[...] = jnp.zeros_like(lg)
    for i in (5, 2, 3, 0, 1, 4):
        local[i].start()

    def drain():
        for cond, src, sem in pending:
            copy = remote(src, src, sem, sem, to_head(sib))
            if cond is None:
                copy.wait_send()
            else:
                pl.when(cond)(copy.wait_send)

    part = feats // (NX * NZ)
    slot = pl.multiple_of((x * NZ + z) * part, part)

    def weights_y():
        local[1].wait()
        mine = w.at[pl.ds(pl.multiple_of(head * feats + slot, part), part), :]
        for d in range(1, 2 * NP):
            other = lax.rem(head + d, 2 * NP)
            remote(
                w.at[pl.ds(pl.multiple_of(other * feats + slot, part), part), :],
                wr.at[head, pl.ds(slot, part), :],
                wy_send.at[0], wy_recv.at[0], to_head(other),
            ).start()
        sent(wr.at[pl.ds(0, 2 * NP - 1), pl.ds(0, part), :], wy_send.at[0])
        wr[head, pl.ds(slot, part), :] = mine[...]

    def weights_z():
        arrived(wr.at[pl.ds(0, 2 * NP - 1), pl.ds(0, part), :], wy_recv.at[0])
        mine = wr.at[:, pl.ds(slot, part), :]
        for d in (4, 3, 5, 2, 6, 1, 7):
            remote(mine, mine, wz_send.at[0], wz_recv.at[0],
                   to_ctx(ctx_at(lax.rem(z + d, NZ), y, x))).start()
        sent(wr.at[:, pl.ds(0, (NZ - 1) * part), :], wz_send.at[0])

    line = part * NZ
    right, left = lax.rem(x + 1, NX), lax.rem(x + NX - 1, NX)
    across = lax.rem(x + 2, NX)

    def line_of(xx):
        return pl.ds(pl.multiple_of(xx * line, line), line)

    def send(src, send_sem, recv_sem, device):
        remote(src, src, send_sem, recv_sem, device).start()
        sent(src, send_sem)

    def weights_x():
        arrived(wr.at[:, pl.ds(0, (NZ - 1) * part), :], wz_recv.at[0])
        mine = wr.at[:, line_of(x), :]
        send(mine, wx_send.at[0], wx_recv.at[0], to_ctx(ctx_at(z, y, right)))
        send(mine, wx_send.at[1], wx_recv.at[1], to_ctx(ctx_at(z, y, left)))

    def weights_forward():
        arrived(wr.at[:, line_of(left), :], wx_recv.at[0])
        half = wr.at[pl.ds(0, NP), line_of(left), :]
        send(half, wf_send.at[0], wf_recv.at[0], to_ctx(ctx_at(z, y, right)))
        arrived(wr.at[:, line_of(right), :], wx_recv.at[1])
        half = wr.at[pl.ds(NP, NP), line_of(right), :]
        send(half, wf_send.at[1], wf_recv.at[1], to_ctx(ctx_at(z, y, left)))

    def weights_end():
        arrived(wr.at[pl.ds(0, NP), line_of(across), :], wf_recv.at[0])
        arrived(wr.at[pl.ds(NP, NP), line_of(across), :], wf_recv.at[1])

    def gather(buf, s_send, s_recv, s_near):
        chunks, groups = s_recv.shape[1], s_near.shape[0]
        step = tokens // chunks
        per = chunks // groups
        targets = []
        for d in OFFSETS:
            other = chip + d
            targets.append((other, jnp.logical_and(other >= 0, other < NP)))
        relays = jnp.logical_and(chip >= 1, chip <= 2)
        end = jnp.where(chip == 2, 3, 0)

        def piece(block, k):
            return buf.at[block, pl.ds(k * step, step), :]

        def issue(k):
            mine = piece(head, k)
            for i, (other, ok) in enumerate(targets):
                pl.when(ok)(remote(mine, mine, s_send.at[i], s_recv.at[chip, k],
                                   to_head(2 * other + core)).start)
            remote(mine, mine, s_send.at[4], s_near.at[k // per], to_head(sib)).start()

        def forward(k):
            for i, d in enumerate((2, 1, 3)):
                source = lax.rem(chip + d, NP)
                got = piece(2 * source + core, k)
                recv = s_recv.at[source, k]
                arrived(got, recv)
                if d == 2:
                    pl.when(relays)(remote(got, got, s_send.at[5], recv,
                                           to_head(2 * end + core)).start)
                remote(got, got, s_send.at[6 + i], s_near.at[k // per], to_head(sib)).start()

        def finish(group):
            arrived(buf.at[pl.ds(0, NP), pl.ds(group * per * step, per * step), :],
                    s_near.at[group])

        def close():
            for i, (_, ok) in enumerate(targets):
                sent(buf.at[head], s_send.at[i], ok)
            sent(buf.at[head], s_send.at[4])
            sent(buf.at[head], s_send.at[5], relays)
            for i in range(3):
                sent(buf.at[head], s_send.at[6 + i])

        return issue, forward, finish, close

    h_issue, h_forward, h_finish, h_close = gather(hid, h_send, h_recv, h_near)
    q_issue, q_forward, q_finish, q_close = gather(dqf, q_send, q_recv, q_near)
    h_step = tokens // h_recv.shape[1]
    q_step = tokens // q_recv.shape[1]

    def line_fold(parts, gains, reverse, start):
        outs = [None] * len(parts)
        acc = start
        order = range(len(parts))
        for i in reversed(order) if reverse else order:
            outs[i] = acc
            acc = [gains[i][h] * acc[h] + parts[i][h] for h in range(nhead)]
        return outs, acc

    def zeros():
        return [jnp.zeros((QUARTER, HDIM), F32) for _ in range(nhead)]

    def gains_of(ref, count):
        return [[jnp.exp(ref[i][h : h + 1, :]) for h in range(nhead)] for i in range(count)]

    def parts_of(ref, n, count):
        return [[ref[n, i, h].astype(F32) for h in range(nhead)] for i in range(count)]

    def scan_x(n, states):
        for q in range(NX):
            for h in range(nhead):
                loc[n, q, h] = states[h][q * QUARTER : (q + 1) * QUARTER].astype(BF16)
        for d in (2, 1, 3):
            xx = lax.rem(x + d, NX)
            device = to_ctx(ctx_at(z, y, xx))
            remote(loc.at[n, xx], p1.at[n, x], s_send.at[n, 0], s_recv.at[n, 0], device).start()
            if n == 0:
                remote(tx.at[x], tx.at[x], t_send.at[0], t_recv.at[0], device).start()
        sent(loc.at[n, pl.ds(0, NX - 1)], s_send.at[n, 0])
        if n == 0:
            sent(tx.at[pl.ds(0, NX - 1)], t_send.at[0])
        p1[n, x] = loc[n, x]

    def scan_y(n):
        arrived(p1.at[n, pl.ds(0, NX - 1)], s_recv.at[n, 0])
        if n == 0:
            arrived(tx.at[pl.ds(0, NX - 1)], t_recv.at[0])
            by[y] = tx[0] + tx[1] + tx[2] + tx[3]
        _, total = line_fold(parts_of(p1, n, NX), gains_of(tx, NX), n == 1, zeros())
        for h in range(nhead):
            p2[n, y, h] = total[h].astype(BF16)
        device = to_ctx(ctx_at(z, 1 - y, x))
        send(p2.at[n, y], s_send.at[n, 1], s_recv.at[n, 1], device)
        if n == 0:
            send(by.at[y], t_send.at[1], t_recv.at[1], device)

    def scan_z(n):
        arrived(p2.at[n, 1 - y], s_recv.at[n, 1])
        if n == 0:
            arrived(by.at[1 - y], t_recv.at[1])
            bz[z] = by[0] + by[1]
        _, total = line_fold(parts_of(p2, n, NY), gains_of(by, NY), n == 1, zeros())
        for h in range(nhead):
            p3[n, z, h] = total[h].astype(BF16)
        for d in (4, 3, 5, 2, 6, 1, 7):
            device = to_ctx(ctx_at(lax.rem(z + d, NZ), y, x))
            remote(p3.at[n, z], p3.at[n, z], s_send.at[n, 2], s_recv.at[n, 2], device).start()
            if n == 0:
                remote(bz.at[z], bz.at[z], t_send.at[2], t_recv.at[2], device).start()
        sent(p3.at[n, pl.ds(0, NZ - 1)], s_send.at[n, 2])
        if n == 0:
            sent(bz.at[pl.ds(0, NZ - 1)], t_send.at[2])

    def scan_back(n):
        arrived(p3.at[n, pl.ds(0, NZ - 1)], s_recv.at[n, 2])
        if n == 0:
            arrived(bz.at[pl.ds(0, NZ - 1)], t_recv.at[2])
        reverse = n == 1
        gains = gains_of(bz, NZ)
        parts = parts_of(p3, n, NZ)
        acc = zeros()
        for i in reversed(range(NZ)) if reverse else range(NZ):
            use = z < i if reverse else z > i
            keep = jnp.where(use, 1.0, 0.0)
            acc = [
                acc[h] * (1.0 - keep + keep * gains[i][h]) + keep * parts[i][h]
                for h in range(nhead)
            ]
        outs, _ = line_fold(parts_of(p2, n, NY), gains_of(by, NY), reverse, acc)
        first = jnp.where(y == 0, 1.0, 0.0)
        acc = [first * outs[0][h] + (1.0 - first) * outs[1][h] for h in range(nhead)]
        outs, _ = line_fold(parts_of(p1, n, NX), gains_of(tx, NX), reverse, acc)
        for i in range(NX):
            for h in range(nhead):
                p4s[n, i, h] = outs[i][h].astype(BF16)
        for d in (2, 1, 3):
            xx = lax.rem(x + d, NX)
            remote(p4s.at[n, xx], p4.at[n, x], s_send.at[n, 3], s_recv.at[n, 3],
                   to_ctx(ctx_at(z, y, xx))).start()
        sent(p4s.at[n, pl.ds(0, NX - 1)], s_send.at[n, 3])
        p4[n, x] = p4s[n, x]

    def scan_end(n):
        arrived(p4.at[n, pl.ds(0, NX - 1)], s_recv.at[n, 3])
        return [
            jnp.concatenate([p4[n, q, h] for q in range(NX)], axis=0) for h in range(nhead)
        ]

    def cols(h):
        return slice(h * HDIM, (h + 1) * HDIM)

    local[5].wait()
    lg[0:nhead, :] = logs[...]
    log_rows = lg[...]
    gate = jnp.sqrt(one_less_exp(2.0 * log_rows))
    lane = lax.broadcasted_iota(jnp.int32, log_rows.shape, 1)
    cumul = log_rows
    shift = 1
    while shift < tokens:
        cumul = cumul + jnp.where(lane >= shift, pltpu.roll(cumul, shift, 1), 0.0)
        shift *= 2
    total = cumul[:, tokens - 1 : tokens]
    tx[x] = jnp.broadcast_to(total, (8, HDIM))
    rows[0:8, :] = gate
    rows[8:16, :] = scale * jnp.exp(cumul)
    rows[16:24, :] = jnp.exp(total - cumul)
    rows[24:32, :] = cumul
    columns = jnp.transpose(rows[...])
    gate_c = [columns[:, h : h + 1] for h in range(nhead)]
    head_c = [columns[:, 8 + h : 9 + h] for h in range(nhead)]
    tail_c = [columns[:, 16 + h : 17 + h] for h in range(nhead)]
    cumul_c = [columns[:, 24 + h : 25 + h] for h in range(nhead)]

    local[2].wait()
    local[3].wait()
    states = []
    for h in range(nhead):
        scaled = (gate_c[h] * keys[:, cols(h)].astype(F32)).astype(BF16)
        sk[:, cols(h)] = scaled
        decayed = (tail_c[h] * scaled.astype(F32)).astype(BF16)
        states.append(mm_tn(decayed, values[:, cols(h)]))

    pl.semaphore_wait(barrier, len(partners))
    weights_y()
    local[0].wait()
    for k in range(AHEAD):
        h_issue(k)
    scan_x(0, states)

    local[4].wait()
    block = 128
    tri = lax.broadcasted_iota(jnp.int32, (block, block), 0) >= lax.broadcasted_iota(
        jnp.int32, (block, block), 1
    )
    for h in range(nhead):
        cumul_r = rows[24 + h : 25 + h, :]
        for t0 in range(0, tokens, block):
            t = slice(t0, t0 + block)
            for s0 in range(0, t0 + block, block):
                s = slice(s0, s0 + block)
                spread = cumul_c[h][t] - cumul_r[:, s]
                if s0 == t0:
                    decays = jnp.where(tri, jnp.exp(jnp.where(tri, spread, 0.0)) * scale, 0.0)
                else:
                    decays = jnp.exp(spread) * scale
                dots = mm_nt(d_out[t, cols(h)], values[s, cols(h)])
                dec[h, t, s] = decays
                wdv[h, t, s] = (decays * dots).astype(BF16)

    def intra_query(h, t0):
        t = slice(t0, t0 + block)
        return mm(wdv[h, t, 0 : t0 + block], sk[0 : t0 + block, cols(h)])

    weights_z()
    scan_y(0)

    def h_product(k0, k1):
        h_finish(k0 // 2)
        t = slice(k0 * h_step, k1 * h_step)
        acc = jnp.zeros((t.stop - t.start, width), F32)
        for b in range(2 * NP):
            acc = acc + mm(hid[b, t, :], w[b * feats : (b + 1) * feats, :])
        query[t, :] = acc.astype(BF16)

    chunks = h_recv.shape[1]

    def h_chunk(k):
        h_forward(k)
        if k + AHEAD < chunks:
            h_issue(k + AHEAD)

    h_chunk(0)
    h_chunk(1)
    scan_z(0)
    h_product(0, 2)
    h_chunk(2)
    weights_x()
    h_chunk(3)
    scan_back(0)
    h_product(2, 4)
    h_chunk(4)
    h_chunk(5)
    h_product(4, 6)

    state_in = scan_end(0)
    for h in range(nhead):
        for t0 in range(0, tokens, block):
            t = slice(t0, t0 + block)
            carry = mm_nt(d_out[t, cols(h)], state_in[h])
            out = intra_query(h, t0) + head_c[h][t] * carry
            dqf[head, t, cols(h)] = out.astype(BF16)

    h_chunk(6)
    h_chunk(7)
    q_issue(0)
    h_product(6, 8)

    adjoints = []
    for h in range(nhead):
        decayed = (head_c[h] * query[:, cols(h)].astype(F32)).astype(BF16)
        adjoints.append(mm_tn(decayed, d_out[:, cols(h)]))
    scan_x(1, adjoints)
    q_chunks = q_recv.shape[1]
    q_issue(1)

    for h in range(nhead):
        for s0 in range(0, tokens, block):
            s = slice(s0, s0 + block)
            later = slice(s0, tokens)
            scores = mm_nt(query[later, cols(h)], sk[s, cols(h)])
            weight = (dec[h, later, s] * scores).astype(BF16)
            sums[0, s, cols(h)] = mm_tn(wdv[h, later, s], query[later, cols(h)])
            sums[1, s, cols(h)] = mm_tn(weight, d_out[later, cols(h)])

    outs = []

    def out_copy(src, dst):
        copy = pltpu.make_async_copy(src, dst, out_sem.at[len(outs)])
        copy.start()
        outs.append(copy)

    def q_product(k):
        q_finish(k)
        t = slice(k * q_step, (k + 1) * q_step)
        acc = jnp.zeros((q_step, feats), F32)
        for b in range(2 * NP):
            acc = acc + mm_nt(dqf[b, t, :], wr[b])
        dh_ref[t, :] = acc.astype(BF16)
        out_copy(dh_ref.at[t, :], dh_hbm.at[t, :])

    scan_y(1)
    for k in range(2, q_chunks):
        q_issue(k)
    weights_forward()
    q_forward(0)
    scan_z(1)
    q_forward(1)
    weights_end()
    q_product(0)
    q_forward(2)
    scan_back(1)
    q_product(1)
    q_forward(3)
    adjoint_in = scan_end(1)
    for h in range(nhead):
        carry_keys = mm_nt(values[:, cols(h)], adjoint_in[h])
        carry_values = mm(sk[:, cols(h)], adjoint_in[h])
        d_scaled = sums[0, :, cols(h)] + tail_c[h] * carry_keys
        dk_ref[:, cols(h)] = (gate_c[h] * d_scaled).astype(BF16)
        dv_ref[:, cols(h)] = (sums[1, :, cols(h)] + tail_c[h] * carry_values).astype(BF16)
    out_copy(dk_ref, dk_hbm)
    out_copy(dv_ref, dv_hbm)
    q_product(2)
    q_product(3)
    h_close()
    q_close()
    drain()
    for copy in outs:
        copy.wait()


def finish(*refs):
    n = 3
    sems = refs[2 * n]
    copies = [pltpu.make_async_copy(refs[i], refs[n + i], sems.at[i]) for i in range(n)]
    for copy in copies:
        copy.start()
    for copy in copies:
        copy.wait()


def body(hidden, w_query, keys, values, d_out, log_decay):
    tokens, feats = hidden.shape
    width = w_query.shape[1]
    nhead = width // HDIM
    groups = 2 * NP
    h_chunks, q_chunks = 8, 4
    dma = pltpu.SemaphoreType.DMA
    vmem = pltpu.VMEM
    scratch = [
        vmem((nhead, tokens), F32),
        vmem((tokens, width), BF16),
        vmem((tokens, width), BF16),
        vmem((tokens, width), BF16),
        vmem((tokens, feats), BF16),
        vmem((tokens, width), BF16),
        vmem((tokens, width), BF16),
        vmem((groups, tokens, feats), BF16),
        vmem(w_query.shape, BF16),
        vmem((groups, feats, width), BF16),
        vmem((groups, tokens, width), BF16),
        vmem((tokens, width), BF16),
        vmem((tokens, width), BF16),
        vmem((8, tokens), F32),
        vmem((128, tokens), F32),
        vmem((nhead, tokens, tokens), F32),
        vmem((nhead, tokens, tokens), BF16),
        vmem((2, NX, nhead, QUARTER, HDIM), BF16),
        vmem((2, NX, nhead, QUARTER, HDIM), BF16),
        vmem((2, NY, nhead, QUARTER, HDIM), BF16),
        vmem((2, NZ, nhead, QUARTER, HDIM), BF16),
        vmem((2, NX, nhead, QUARTER, HDIM), BF16),
        vmem((2, NX, nhead, QUARTER, HDIM), BF16),
        vmem((NX, 8, HDIM), F32),
        vmem((NY, 8, HDIM), F32),
        vmem((NZ, 8, HDIM), F32),
        vmem((2, tokens, width), F32),
        dma((6,)),
        dma((q_chunks + 2,)),
    ]
    for chunks in (h_chunks, q_chunks):
        scratch += [dma((9,)), dma((NP, chunks)), dma((4,))]
    scratch += [dma((1,))] * 4 + [dma((2,))] * 4
    scratch += [dma((2, 4)), dma((2, 4)), dma((3,)), dma((3,))]
    anywhere = pl.BlockSpec(memory_space=pl.ANY)
    shapes = (
        jax.ShapeDtypeStruct((tokens, feats), BF16),
        jax.ShapeDtypeStruct((tokens, width), BF16),
        jax.ShapeDtypeStruct((tokens, width), BF16),
    )
    results = pl.pallas_call(
        kernel,
        out_shape=shapes,
        in_specs=[pl.BlockSpec(memory_space=pltpu.HBM)] * 6,
        out_specs=(anywhere,) * 3,
        scratch_shapes=scratch,
        compiler_params=pltpu.CompilerParams(
            collective_id=0, has_side_effects=True, vmem_limit_bytes=32 * 1024 * 1024
        ),
    )(*(pltpu.with_memory_space_constraint(a, pltpu.HBM) for a in (hidden, w_query, keys, values, d_out, log_decay.T)))
    return pl.pallas_call(
        finish,
        out_shape=shapes,
        in_specs=[anywhere] * 3,
        out_specs=(anywhere,) * 3,
        scratch_shapes=[dma((3,))],
        compiler_params=pltpu.CompilerParams(vmem_limit_bytes=4 * 1024 * 1024),
    )(*results)


def solution(mesh):
    return jax.shard_map(
        body,
        mesh=mesh,
        in_specs=(
            P("ctx", "head"),
            P(None, "head"),
            P("ctx", "head"),
            P("ctx", "head"),
            P("ctx", "head"),
            P("ctx", "head"),
        ),
        out_specs=(P("ctx", "head"), P("ctx", "head"), P("ctx", "head")),
        check_vma=False,
    )
```

time: 89.4 us -> 78.3 us (0.88)
  Pallas kernels: 83.3 us -> 77.5 us
  local copies, waits for them, and re-layouts: 5.21 us -> 0 us
    pallas_call x1 -> x2, Pallas kernels: 83.3 us -> 77.5 us  [the longest x1 76.5 us: body(): pl.pallas_call(kernel, out_shape=shapes, in_specs=[pl.BlockSpec(memory_sp...]
    unnamed x3 -> x0, local copies, waits for them, and re-layouts: 5.21 us -> none
where the time goes in v2:
time: 78.3 us; the launch traced here: 78.1 us
  Pallas kernels  77.5 us (99%)
    pallas_call x1, Pallas kernels, body(): pl.pallas_call(kernel, out_shape=shapes, in_specs=[pl.BlockSpec(memory_sp...  76.5 us

profile of v2, /device:TPU:1, one launch (start us, length us, event | category | flops | bytes accessed | tf_op | source)
XLA Modules:
  0.0 78.1 jit_solution(16395978616247258177)
XLA Ops:
  0.6 76.5 %shard_map.85 = (bf16[512,512]{1,0:T(8,128)(2,1)S(1)}, bf16[512,256]{1,0:T(8,128)(2,1)S(1)}, bf16[512,256]{1,0:T(8,128)(2,1)S(1)}) custom-call(bf16[512,512]{1,0:T(8,128)(2,1)} %hidden.1, bf16[4096,256]{1,0:T(8,128)(2,1)} %w_hbm.1, bf16[512,256]{1,0:T(8,128)(2,1)} %keys_hbm.1, bf16[512,256]{1,0:T(8,128)(2,1)} %values_hbm.1, bf16[512,256]{1,0:T(8,128)(2,1)} %d_out_hbm.1, ...), custom_call_target="tpu_custom_call" | custom-call | tf_op jit(solution)/shard_map/pallas_call | solution.py:548
  77.2 1.0 %shard_map.86 = (bf16[512,512]{1,0:T(8,128)(2,1)}, bf16[512,256]{1,0:T(8,128)(2,1)}, bf16[512,256]{1,0:T(8,128)(2,1)}) custom-call(bf16[512,512]{1,0:T(8,128)(2,1)S(1)} %get-tuple-element.6.refs_0_, bf16[512,256]{1,0:T(8,128)(2,1)S(1)} %get-tuple-element.7.refs_1_, bf16[512,256]{1,0:T(8,128)(2,1)S(1)} %get-tuple-element.8.refs_2_), custom_call_target="tpu_custom_call" | custom-call | tf_op jit(solution)/shard_map/pallas_call | solution.py:558

commit v3 on v2

--- a/solution.py
+++ b/solution.py
@@ -15,7 +15,7 @@
 NP = 4
 QUARTER = HDIM // NX
 OFFSETS = (2, -2, 1, -1)
-AHEAD = 3
+AHEAD = (4, 2)
 
 
 def mm(a, b):
@@ -350,8 +350,16 @@
     pl.semaphore_wait(barrier, len(partners))
     weights_y()
     local[0].wait()
-    for k in range(AHEAD):
-        h_issue(k)
+    def h_issue_by(which, k):
+        if k < chunks:
+            @pl.when(core == which)
+            def _():
+                h_issue(k)
+
+    chunks = h_recv.shape[1]
+    for which, ahead in enumerate(AHEAD):
+        for k in range(ahead):
+            h_issue_by(which, k)
     scan_x(0, states)
 
     local[4].wait()
@@ -389,12 +397,10 @@
             acc = acc + mm(hid[b, t, :], w[b * feats : (b + 1) * feats, :])
         query[t, :] = acc.astype(BF16)
 
-    chunks = h_recv.shape[1]
-
     def h_chunk(k):
         h_forward(k)
-        if k + AHEAD < chunks:
-            h_issue(k + AHEAD)
+        for which, ahead in enumerate(AHEAD):
+            h_issue_by(which, k + ahead)
 
     h_chunk(0)
     h_chunk(1)
@@ -430,6 +436,27 @@
     q_chunks = q_recv.shape[1]
     q_issue(1)
 
+    outs = []
+
+    def out_copy(src, dst):
+        copy = pltpu.make_async_copy(src, dst, out_sem.at[len(outs)])
+        copy.start()
+        outs.append(copy)
+
+    def q_product(k):
+        q_finish(k)
+        t = slice(k * q_step, (k + 1) * q_step)
+        acc = jnp.zeros((q_step, feats), F32)
+        for b in range(2 * NP):
+            acc = acc + mm_nt(dqf[b, t, :], wr[b])
+        dh_ref[t, :] = acc.astype(BF16)
+        out_copy(dh_ref.at[t, :], dh_hbm.at[t, :])
+
+    scan_y(1)
+    for k in range(2, q_chunks):
+        q_issue(k)
+    weights_forward()
+
     for h in range(nhead):
         for s0 in range(0, tokens, block):
             s = slice(s0, s0 + block)
@@ -439,35 +466,16 @@
             sums[0, s, cols(h)] = mm_tn(wdv[h, later, s], query[later, cols(h)])
             sums[1, s, cols(h)] = mm_tn(weight, d_out[later, cols(h)])
 
-    outs = []
-
-    def out_copy(src, dst):
-        copy = pltpu.make_async_copy(src, dst, out_sem.at[len(outs)])
-        copy.start()
-        outs.append(copy)
-
-    def q_product(k):
-        q_finish(k)
-        t = slice(k * q_step, (k + 1) * q_step)
-        acc = jnp.zeros((q_step, feats), F32)
-        for b in range(2 * NP):
-            acc = acc + mm_nt(dqf[b, t, :], wr[b])
-        dh_ref[t, :] = acc.astype(BF16)
-        out_copy(dh_ref.at[t, :], dh_hbm.at[t, :])
-
-    scan_y(1)
-    for k in range(2, q_chunks):
-        q_issue(k)
-    weights_forward()
     q_forward(0)
     scan_z(1)
     q_forward(1)
+    q_forward(2)
+    scan_back(1)
     weights_end()
     q_product(0)
-    q_forward(2)
-    scan_back(1)
+    q_forward(3)
     q_product(1)
-    q_forward(3)
+    q_product(2)
     adjoint_in = scan_end(1)
     for h in range(nhead):
         carry_keys = mm_nt(values[:, cols(h)], adjoint_in[h])
@@ -477,7 +485,6 @@
         dv_ref[:, cols(h)] = (sums[1, :, cols(h)] + tail_c[h] * carry_values).astype(BF16)
     out_copy(dk_ref, dk_hbm)
     out_copy(dv_ref, dv_hbm)
-    q_product(2)
     q_product(3)
     h_close()
     q_close()

time: 78.3 us -> 78.2 us (level)
  no operation moved by 1% of the time
where the time goes in v3:
time: 78.2 us; the launch traced here: 78.1 us
  Pallas kernels  77.4 us (99%)
    pallas_call x1, Pallas kernels, body(): pl.pallas_call(kernel, out_shape=shapes, in_specs=[pl.BlockSpec(memory_sp...  76.4 us

profile of v3, /device:TPU:1, one launch (start us, length us, event | category | flops | bytes accessed | tf_op | source)
XLA Modules:
  0.0 78.1 jit_solution(16308111721379031395)
XLA Ops:
  0.6 76.4 %shard_map.85 = (bf16[512,512]{1,0:T(8,128)(2,1)S(1)}, bf16[512,256]{1,0:T(8,128)(2,1)S(1)}, bf16[512,256]{1,0:T(8,128)(2,1)S(1)}) custom-call(bf16[512,512]{1,0:T(8,128)(2,1)} %hidden.1, bf16[4096,256]{1,0:T(8,128)(2,1)} %w_hbm.1, bf16[512,256]{1,0:T(8,128)(2,1)} %keys_hbm.1, bf16[512,256]{1,0:T(8,128)(2,1)} %values_hbm.1, bf16[512,256]{1,0:T(8,128)(2,1)} %d_out_hbm.1, ...), custom_call_target="tpu_custom_call" | custom-call | tf_op jit(solution)/shard_map/pallas_call | solution.py:555
  77.1 1.0 %shard_map.86 = (bf16[512,512]{1,0:T(8,128)(2,1)}, bf16[512,256]{1,0:T(8,128)(2,1)}, bf16[512,256]{1,0:T(8,128)(2,1)}) custom-call(bf16[512,512]{1,0:T(8,128)(2,1)S(1)} %get-tuple-element.6.refs_0_, bf16[512,256]{1,0:T(8,128)(2,1)S(1)} %get-tuple-element.7.refs_1_, bf16[512,256]{1,0:T(8,128)(2,1)S(1)} %get-tuple-element.8.refs_2_), custom_call_target="tpu_custom_call" | custom-call | tf_op jit(solution)/shard_map/pallas_call | solution.py:565
